TPU v7x, 256 devices: a whole 4x4x8 slice. The times are simulated.
256 devices in a mesh: gx: 4 (over y_lo, core), gy: 64 (over y_hi, x, z).
Axes of the slice: x: 4, y: 4 (y_hi: 2, y_lo: 2; y = y_hi * 2 + y_lo), z: 8, core: 2. Of those that a mesh axis runs over, the one named last changes fastest.
Arguments:
- hidden: bfloat16 [8192, 2048], P('gy', 'gx'), may hold values from -6 to 6
- segment_ids: int32 [8192], replicated, may hold values from 0 to 31, never falling along the last dimension, each value on 1 to 4352 neighbouring positions
- expert_ids: int32 [8192, 6], P('gy'), may hold values from 0 to 63, all different within a row; in each aligned block of 128 rows (0 to 127, 128 to 255, ...) at most 15 rows name the same one
- route_weight: float32 [8192, 6], P('gy'), may hold values from 0.1 to 1
- attn_gain: float32 [2048], replicated, may hold values from 0.1 to 1.9
- kv_gain: float32 [512], replicated, may hold values from 0.1 to 1.9
- ffn_gain: float32 [2048], replicated, may hold values from 0.1 to 1.9
- w_q: bfloat16 [2048, 3072], P('gy', 'gx'), may hold values from -2 to 2
- w_kv_a: bfloat16 [2048, 576], P('gy', 'gx'), may hold values from -0.125 to 0.125
- w_kv_b: bfloat16 [512, 4096], P('gy', 'gx'), may hold values from -0.25 to 0.25
- w_o: bfloat16 [2048, 2048], P('gx', 'gy'), may hold values from -0.125 to 0.125
- w_gate: bfloat16 [64, 2048, 1408], P('gy', None, 'gx'), may hold values from -0.125 to 0.125
- w_up: bfloat16 [64, 2048, 1408], P('gy', None, 'gx'), may hold values from -0.125 to 0.125
- w_down: bfloat16 [64, 1408, 2048], P('gy', 'gx'), may hold values from -0.15625 to 0.15625
- page_table: int32 [512], P(('gx', 'gy')), may hold values from 0 to 511, each once
Outputs:
- output: bfloat16 [8192, 2048], P('gy', 'gx')
- latent_cache: bfloat16 [512, 16, 576], P(('gx', 'gy'))
Inputs may be any that keep to these rules, and one draw needn't show every extreme that they name: `segment_ids`: never falling along the stream; every prompt has 1 to 4352 tokens and one has exactly 4352. `expert_ids`: a token names 6 different experts; among the rows of one index of gy no expert is named by more than 15 rows, and in some of them one expert is named by exactly 15. `page_table`: a permutation of the stream's pages.
All inputs are finite; a program needn't handle non-finite values.
Results may differ from a plain program's by a relative error of at most 0.014.
The roundings to bfloat16 on the way count: a program that leaves them out, or rounds other values in their place, can miss the bound.
Values may be sent and summed in bfloat16 or wider, within the bound.
No kernel may reach another device: no remote copies, remote signals or barrier semaphores. Data moves between devices by JAX's collectives and lax.ppermute only.
A program may use at most 128 MiB of HBM per device.

v0:
```python
import jax
import jax.numpy as jnp
from jax import lax
from jax.experimental import pallas as pl
from jax.experimental.pallas import tpu as pltpu
from jax.sharding import Mesh, PartitionSpec as P


NOPE = 128
ROPE = 64
VDIM = 128
RANK = 512
PAGE = 16
KEY = RANK + ROPE
WIDE = 640

GX = ("yl", "c")
GY = ("yh", "x", "z")
YL, CORES, YH, XS, ZS = 2, 2, 2, 4, 8
GROUPS = YH * XS * ZS
PARTS = YL * CORES
SLOTS = 16
SWAP = [(0, 1), (1, 0)]

eps = 1e-06
masked_score = -1e30


def norm_rows(values, gain):
    mean_sq = jnp.mean(values * values, axis=-1, keepdims=True)
    return values * lax.rsqrt(mean_sq + eps) * gain


def angle_table(positions, width):
    exponents = jnp.arange(width // 2, dtype=jnp.float32) * (2.0 / width)
    freqs = jnp.power(10000.0, -exponents)
    return positions.astype(jnp.float32)[:, None] * freqs[None, :]


def rotate(values, cosine, sine):
    half = values.shape[-1] // 2
    first = values[..., :half]
    second = values[..., half:]
    return jnp.concatenate(
        [first * cosine - second * sine, second * cosine + first * sine], axis=-1
    )


def shift(values, axis, size, step):
    return lax.ppermute(values, axis, [(i, (i + step) % size) for i in range(size)])


def swap(values, axis):
    return lax.ppermute(values, axis, SWAP)


def spread(values, axis, size):
    blocks = jnp.broadcast_to(values[None], (size,) + values.shape)
    return lax.all_to_all(blocks, axis, split_axis=0, concat_axis=0, tiled=True)


def attention_kernel(
    meta, q_ref, qlo_ref, qpos_ref, a_own, a_oth, b_own, b_oth, wuv_ref, out_ref,
    best, total, accum,
):
    step = pl.program_id(0)
    kmin, kmax, core = meta[16], meta[17], meta[18]

    @pl.when(step == 0)
    def _():
        best[...] = jnp.full_like(best, masked_score)
        total[...] = jnp.zeros_like(total)
        accum[...] = jnp.zeros_like(accum)

    def block(base, colour, own_ref, oth_ref):
        @pl.when((base <= kmax) & (base + 1023 >= kmin))
        def _():
            queries = q_ref[...]
            lo, hi = qlo_ref[...], qpos_ref[...]
            row = lax.broadcasted_iota(jnp.int32, (1, 256), 1)
            place = base + (row // 32) * 128 + row % 32 + colour * 32
            scores, masks = [], []
            for ref, side in ((own_ref, core), (oth_ref, 1 - core)):
                keys = ref[0]
                raw = lax.dot_general(
                    queries, keys, (((1,), (1,)), ((), ())), preferred_element_type=jnp.float32
                )
                where = place + side * 64
                mask = (where >= lo) & (where <= hi)
                scores.append(jnp.where(mask, raw, masked_score))
                masks.append(mask)
            old = best[...]
            new = jnp.maximum(
                old,
                jnp.maximum(
                    jnp.max(scores[0], axis=-1, keepdims=True),
                    jnp.max(scores[1], axis=-1, keepdims=True),
                ),
            )
            alpha = jnp.exp(old - new)
            best[...] = new
            grown = total[...] * alpha
            fresh = accum[...] * alpha
            for ref, score, mask in ((own_ref, scores[0], masks[0]), (oth_ref, scores[1], masks[1])):
                weight = jnp.where(mask, jnp.exp(score - new), 0.0)
                grown = grown + jnp.sum(weight, axis=-1, keepdims=True)
                fresh = fresh + jnp.dot(
                    weight.astype(jnp.bfloat16), ref[0, :, :RANK],
                    preferred_element_type=jnp.float32,
                )
            total[...] = grown
            accum[...] = fresh

    block(meta[step], 0, a_own, a_oth)
    block(meta[8 + step], 1, b_own, b_oth)

    @pl.when(step == pl.num_programs(0) - 1)
    def _():
        rows = out_ref.shape[0]
        mixed = (accum[...] / total[...]).astype(jnp.bfloat16)
        for h in range(wuv_ref.shape[0]):
            out_ref[:, h * VDIM : (h + 1) * VDIM] = jnp.dot(
                mixed[h * rows : (h + 1) * rows], wuv_ref[h], preferred_element_type=jnp.float32
            ).astype(jnp.bfloat16)


def project_kernel(heads_ref, wo_ref, out_ref):
    heads = heads_ref[...]
    crowds = wo_ref.shape[1] // PARTS
    for part in range(PARTS):
        rows = jnp.concatenate(
            [
                wo_ref[z, part * crowds + j]
                for j in range(crowds)
                for z in range(wo_ref.shape[0])
            ],
            axis=0,
        )
        out_ref[part // CORES, part % CORES] = lax.dot_general(
            heads, rows, (((1,), (1,)), ((), ())), preferred_element_type=jnp.float32
        )


def project(heads_out, out_rows):
    zs, crowd, depth, _ = out_rows.shape
    width = zs * crowd * depth // PARTS
    return pl.pallas_call(
        project_kernel,
        out_shape=jax.ShapeDtypeStruct(
            (YL, CORES, heads_out.shape[0], width), jnp.float32
        ),
        in_specs=[pl.BlockSpec(memory_space=pltpu.VMEM)] * 2,
        out_specs=pl.BlockSpec(memory_space=pltpu.VMEM),
        cost_estimate=pl.CostEstimate(
            flops=270_000_000, bytes_accessed=3_000_000, transcendentals=0
        ),
        compiler_params=pltpu.CompilerParams(vmem_limit_bytes=24 << 20),
    )(heads_out, out_rows)


def attention(meta, queries, qlo, qpos, keys, w_uv):
    head_rows = queries.shape[0]
    rows = head_rows // w_uv.shape[0]
    out_dims = (rows, w_uv.shape[0] * VDIM)

    def whole(shape):
        return pl.BlockSpec(shape, lambda i, m: (0,) * len(shape))

    key_spec = pl.BlockSpec((1, 256, WIDE), lambda i, m: (i, 0, 0))
    return pl.pallas_call(
        attention_kernel,
        out_shape=jax.ShapeDtypeStruct(out_dims, jnp.bfloat16),
        grid_spec=pltpu.PrefetchScalarGridSpec(
            num_scalar_prefetch=1,
            grid=(8,),
            in_specs=[
                whole(queries.shape), whole(qlo.shape), whole(qpos.shape),
                key_spec, key_spec, key_spec, key_spec,
                whole(w_uv.shape),
            ],
            out_specs=whole(out_dims),
            scratch_shapes=[
                pltpu.VMEM((head_rows, 1), jnp.float32),
                pltpu.VMEM((head_rows, 1), jnp.float32),
                pltpu.VMEM((head_rows, RANK), jnp.float32),
            ],
        ),
        cost_estimate=pl.CostEstimate(
            flops=9_000_000_000, bytes_accessed=16_000_000, transcendentals=4_000_000
        ),
        compiler_params=pltpu.CompilerParams(
            dimension_semantics=("arbitrary",), vmem_limit_bytes=40 << 20
        ),
    )(meta, queries, qlo, qpos, *keys, w_uv)


def expert_kernel(
    order, own_ref, oth_ref, wg0, wu0, wd0, wg1, wu1, wd1, kept_ref, given_ref
):
    share = own_ref.shape[2]
    across = (((1,), (1,)), ((), ()))
    starts = [pl.multiple_of(order[j] * share, share) for j in range(4)]
    pieces = [own_ref[0], own_ref[1], oth_ref[0], oth_ref[1]]
    actives = []
    for wg_ref, wu_ref in ((wg0, wu0), (wg1, wu1)):
        gate = jnp.zeros((pieces[0].shape[0], wg_ref.shape[0]), jnp.float32)
        upper = gate
        for start, piece in zip(starts, pieces):
            gate = gate + lax.dot_general(
                piece, wg_ref[:, pl.ds(start, share)], across,
                preferred_element_type=jnp.float32,
            )
            upper = upper + lax.dot_general(
                piece, wu_ref[:, pl.ds(start, share)], across,
                preferred_element_type=jnp.float32,
            )
        actives.append((gate / (1.0 + jnp.exp(-gate)) * upper).astype(jnp.bfloat16))
    for j, start in enumerate(starts):
        parts = [
            jnp.dot(active, wd_ref[:, pl.ds(start, share)], preferred_element_type=jnp.float32)
            .astype(jnp.bfloat16)
            .astype(jnp.float32)
            for active, wd_ref in zip(actives, (wd0, wd1))
        ]
        target = kept_ref if j < 2 else given_ref
        target[j % 2] = (parts[0] + parts[1]).astype(target.dtype)


def experts(order, own, oth, *weights):
    _, count, share = own.shape
    tile = 256

    def whole(shape):
        return pl.BlockSpec(shape, lambda i, m: (0,) * len(shape))

    row_spec = pl.BlockSpec((2, tile, share), lambda i, m: (0, i, 0))
    return pl.pallas_call(
        expert_kernel,
        out_shape=[
            jax.ShapeDtypeStruct(own.shape, jnp.float32),
            jax.ShapeDtypeStruct(own.shape, jnp.bfloat16),
        ],
        grid_spec=pltpu.PrefetchScalarGridSpec(
            num_scalar_prefetch=1,
            grid=(count // tile,),
            in_specs=[row_spec] * 2 + [whole(w.shape) for w in weights],
            out_specs=[row_spec] * 2,
        ),
        cost_estimate=pl.CostEstimate(
            flops=4_400_000_000, bytes_accessed=14_000_000, transcendentals=400_000
        ),
        compiler_params=pltpu.CompilerParams(
            dimension_semantics=("arbitrary",), vmem_limit_bytes=48 << 20
        ),
    )(order, own, oth, *weights)


def layer(
    hidden, segment_ids, expert_ids, route_weight, attn_gain, kv_gain, ffn_gain,
    w_q, w_kv_a, w_kv_b, w_o, w_gate, w_up, w_down, page_table,
):
    row_count, share = hidden.shape
    yl, core = lax.axis_index("yl"), lax.axis_index("c")
    yh, x, z = (lax.axis_index(name) for name in GY)
    row_start = ((yh * XS + x) * ZS + z) * row_count
    head_count = w_q.shape[1] // (NOPE + ROPE)
    depth = w_q.shape[0]

    expand_rows = w_kv_b.shape[0]
    local_expand = (
        w_kv_b.reshape(expand_rows, head_count, NOPE + VDIM)
        .transpose(1, 0, 2)
        .reshape(expand_rows * head_count, NOPE + VDIM)
    )
    packed = jnp.concatenate([w_q, local_expand, w_o.T], axis=1)
    crowd, late = YH * XS, packed.shape[1]
    tail_cols = w_kv_a.shape[1] - 128
    latent_packed = jnp.concatenate(
        [w_kv_a[:, :128], w_kv_a[:, 128:].reshape(depth * tail_cols // 128, 128)], axis=0
    )
    latent_all = spread(latent_packed, GY, GROUPS)
    latent_main = latent_all[:, :depth].reshape(GROUPS * depth, 128)
    latent_tail = latent_all[:, depth:].reshape(GROUPS * depth, tail_cols)
    w1, w2, w3 = (shift(packed[None], "x", XS, k) for k in range(1, XS))
    circle = jnp.concatenate([w3, w2, w1, packed[None], w3, w2, w1], axis=0)
    along_x = lax.dynamic_slice_in_dim(circle, XS - 1 - x, XS)
    across_yh = swap(along_x, "yh")
    near_weights = jnp.where(
        yh == 0,
        jnp.concatenate([along_x, across_yh], axis=0),
        jnp.concatenate([across_yh, along_x], axis=0),
    )
    positions = row_start + jnp.arange(row_count, dtype=jnp.int32)
    own_segments = lax.dynamic_slice_in_dim(segment_ids, row_start, row_count)
    prompt_start = jnp.sum(
        (segment_ids[None, :] < own_segments[:, None]).astype(jnp.int32), axis=1
    )
    angles = angle_table(positions - prompt_start, ROPE)
    cosine, sine = jnp.cos(angles), jnp.sin(angles)

    full_rows = lax.all_gather(hidden, GX, axis=1, tiled=True)
    normed = norm_rows(full_rows.astype(jnp.float32), attn_gain).astype(jnp.bfloat16)

    gate_t, up_t, down = w_gate[0].T, w_up[0].T, w_down[0]
    gate_far = swap(gate_t, "yl")
    up_far = swap(up_t, "yl")
    down_far = swap(down, "yl")

    kv_part = jnp.concatenate(
        [
            jnp.dot(normed, latent_main, preferred_element_type=jnp.float32),
            jnp.dot(normed, latent_tail, preferred_element_type=jnp.float32),
        ],
        axis=1,
    )
    kv_raw = lax.all_gather(kv_part, GX, axis=1, tiled=True)
    half = row_count // CORES
    kv_half = lax.dynamic_slice_in_dim(kv_raw, core * half, half)
    keys = jnp.concatenate(
        [
            norm_rows(kv_half[:, :RANK], kv_gain),
            rotate(
                kv_half[:, RANK:],
                lax.dynamic_slice_in_dim(cosine, core * half, half),
                lax.dynamic_slice_in_dim(sine, core * half, half),
            ),
            jnp.zeros((half, WIDE - KEY), jnp.float32),
        ],
        axis=1,
    ).astype(jnp.bfloat16)
    along_z = spread(keys, "z", ZS)
    near_weights = near_weights + along_z[0, 0, 0] * 0
    front_cols = w_q.shape[1] + NOPE + VDIM
    weights = (
        lax.all_gather(
            near_weights[:, :, :front_cols].reshape(crowd * depth, front_cols), "z",
            axis=0, tiled=True,
        )
        .reshape(ZS, crowd, depth, front_cols)
        .transpose(1, 0, 2, 3)
        .reshape(GROUPS * depth, front_cols)
    )
    out_rows = lax.all_gather(
        near_weights[:, :, front_cols:].reshape(crowd * depth, late - front_cols), "z",
        axis=0, tiled=True,
    ).reshape(ZS, crowd, depth, late - front_cols)
    quarter = half // 2
    a0 = along_z[:, :quarter].reshape(1, ZS * quarter, WIDE)
    b0 = along_z[:, quarter:].reshape(1, ZS * quarter, WIDE)
    b1 = jnp.concatenate([b0, swap(b0, "yh")], axis=0)
    a1 = jnp.concatenate([a0] + [shift(a0, "x", XS, k) for k in range(1, XS)], axis=0)
    a_own = jnp.concatenate([a1, swap(a1, "yh")], axis=0)
    b_own = jnp.concatenate([b1] + [shift(b1, "x", XS, k) for k in range(1, XS)], axis=0)
    a_oth = swap(a_own, "c")
    b_oth = swap(b_own, "c")
    steps = jnp.arange(8, dtype=jnp.int32)
    base_a = ((yh ^ (steps // 4)) * XS + (x - steps % 4) % XS) * (ZS * row_count)
    base_b = ((yh ^ (steps % 2)) * XS + (x - steps // 2) % XS) * (ZS * row_count)
    meta = jnp.concatenate(
        [
            base_a, base_b,
            jnp.stack([prompt_start[0], row_start + row_count - 1, core]).astype(jnp.int32),
        ]
    ).astype(jnp.int32)

    pages = []
    for i in range(page_table.shape[0]):
        page = page_table[i]
        group, inside = page // (row_count // PAGE), page % (row_count // PAGE)
        far_yh, far_x = (group // (XS * ZS)) ^ yh, (x - (group // ZS) % XS) % XS
        start = (group % ZS) * quarter + (inside % 2) * PAGE
        is_own = inside // 4 == core
        index_a, index_b = far_yh * XS + far_x, far_x * YH + far_yh
        size = (1, PAGE, WIDE)
        from_a = jnp.where(
            is_own,
            lax.dynamic_slice(a_own, (index_a, start, 0), size),
            lax.dynamic_slice(a_oth, (index_a, start, 0), size),
        )
        from_b = jnp.where(
            is_own,
            lax.dynamic_slice(b_own, (index_b, start, 0), size),
            lax.dynamic_slice(b_oth, (index_b, start, 0), size),
        )
        pages.append(jnp.where((inside % 4) // 2 == 0, from_a, from_b))
    latent_cache = jnp.concatenate(pages, axis=0)[:, :, :KEY]

    q_cols = w_q.shape[1]
    expand = (
        weights[:, q_cols : q_cols + NOPE + VDIM]
        .reshape(GROUPS, head_count, expand_rows, NOPE + VDIM)
        .transpose(1, 0, 2, 3)
        .reshape(head_count, RANK, NOPE + VDIM)
    )
    scale = (NOPE + ROPE) ** (-0.5)
    query = jnp.dot(normed, weights[:, :q_cols], preferred_element_type=jnp.float32).reshape(
        row_count, head_count, NOPE + ROPE
    )
    q_nope = query[:, :, :NOPE].astype(jnp.bfloat16)
    absorbed = (
        jnp.einsum("thn,hrn->htr", q_nope, expand[:, :, :NOPE], preferred_element_type=jnp.float32)
        * scale
    ).astype(jnp.bfloat16)
    rotated = (
        rotate(query[:, :, NOPE:], cosine[:, None, :], sine[:, None, :]) * scale
    ).astype(jnp.bfloat16)
    blank = jnp.zeros((head_count, row_count, WIDE - KEY), jnp.bfloat16)
    queries = jnp.concatenate(
        [absorbed, jnp.transpose(rotated, (1, 0, 2)), blank], axis=2
    ).reshape(head_count * row_count, WIDE)
    qlo = jnp.tile(prompt_start.astype(jnp.int32), head_count)[:, None]
    qpos = jnp.tile(positions, head_count)[:, None]
    heads_out = attention(
        meta, queries, qlo, qpos, (a_own, a_oth, b_own, b_oth), expand[:, :, NOPE:]
    )
    head_terms = project(heads_out, out_rows)

    kept = lax.dynamic_index_in_dim(head_terms, core, 1, keepdims=False)
    given = lax.dynamic_index_in_dim(head_terms, 1 - core, 1, keepdims=False)
    pair_sum = kept + swap(given, "c")
    mine = lax.dynamic_index_in_dim(pair_sum, yl, 0, keepdims=False)
    theirs = lax.dynamic_index_in_dim(pair_sum, 1 - yl, 0, keepdims=False)
    head_sum = mine + swap(theirs, "yl")
    residual = (hidden.astype(jnp.float32) + head_sum).astype(jnp.bfloat16)
    wide = residual.astype(jnp.float32)
    squares = lax.all_gather(jnp.sum(wide * wide, axis=1)[None], GX, axis=0, tiled=True)
    mean_sq = jnp.sum(squares, axis=0)[:, None] * (1.0 / (share * PARTS))
    own_gain = lax.dynamic_slice_in_dim(ffn_gain, (yl * CORES + core) * share, share)
    ffn_in = (wide * lax.rsqrt(mean_sq + eps) * own_gain).astype(jnp.bfloat16)

    top_count = expert_ids.shape[1]
    expert_range = jnp.arange(GROUPS, dtype=jnp.int32)
    chosen = (expert_ids[:, :, None] == expert_range).astype(jnp.float32)
    named = jnp.sum(chosen, axis=1)
    earlier = (
        jnp.arange(row_count)[:, None] > jnp.arange(row_count)[None, :]
    ).astype(jnp.float32)
    before = jnp.dot(earlier, named, preferred_element_type=jnp.float32)
    ranks = jnp.sum(chosen * before[:, None, :], axis=2).astype(jnp.int32)
    slots = expert_ids * SLOTS + ranks
    order = jnp.stack([core, 2 + core, 1 - core, 3 - core]).astype(jnp.int32)
    chunk = SLOTS // YL
    group_rows = GROUPS * chunk
    counter = jnp.arange(YL * group_rows, dtype=jnp.int32)
    slot_range = counter % group_rows // chunk * SLOTS + counter % chunk + counter // group_rows * chunk
    pick = jnp.zeros((YL * group_rows, row_count), jnp.bool_)
    blend = jnp.zeros((row_count, YL * group_rows), jnp.float32)
    for k in range(top_count):
        pick = pick | (slot_range[:, None] == slots[:, k][None, :])
        blend = blend + jnp.where(
            slots[:, k][:, None] == slot_range[None, :], route_weight[:, k][:, None], 0.0
        )
    outgoing = jnp.dot(
        pick.astype(jnp.bfloat16), ffn_in, preferred_element_type=jnp.float32
    ).astype(jnp.bfloat16)
    incoming = lax.all_to_all(
        outgoing.reshape(YL * GROUPS, chunk, share), ("yl",) + GY,
        split_axis=0, concat_axis=0, tiled=True,
    ).reshape(YL, group_rows, share)
    kept, given = experts(
        order, incoming, swap(incoming, "c"), gate_t, up_t, down, gate_far, up_far, down_far
    )
    summed = (kept + swap(given, "c").astype(jnp.float32)).astype(jnp.bfloat16)
    returned = lax.all_to_all(
        summed.reshape(YL * GROUPS, chunk, share), ("yl",) + GY,
        split_axis=0, concat_axis=0, tiled=True,
    ).reshape(YL * group_rows, share)
    moe = jnp.dot(
        blend, returned.astype(jnp.float32), precision=lax.Precision.HIGHEST,
        preferred_element_type=jnp.float32,
    )
    output = (residual.astype(jnp.float32) + moe).astype(jnp.bfloat16)
    return (output, latent_cache)


def solution(mesh):
    fine = Mesh(mesh.devices.reshape(YL, CORES, YH, XS, ZS), GX + GY)
    return jax.shard_map(
        layer,
        mesh=fine,
        in_specs=(
            P(GY, GX),
            P(),
            P(GY, None),
            P(GY, None),
            P(),
            P(),
            P(),
            P(GY, GX),
            P(GY, GX),
            P(GY, GX),
            P(GX, GY),
            P(GY, None, GX),
            P(GY, None, GX),
            P(GY, GX, None),
            P(GX + GY),
        ),
        out_specs=(P(GY, GX), P(GX + GY, None, None)),
        check_vma=False,
    )
```

profile of v0, /device:TPU:38, one launch (start us, length us, event | category | flops | bytes accessed | tf_op | source)
XLA Modules:
  0.0 380.7 jit_solution(6229039472847465605)
XLA Ops:
  8.6 2.4 collective-permute-start.1
  13.4 14.6 %all-to-all-start = ((bf16[64,36,128]{2,1,0:T(8,128)(2,1)}), bf16[64,36,128]{2,1,0:T(8,128)(2,1)S(1)}, u32[]{:S(2)}, u32[]{:S(2)}) async-start(bf16[64,36,128]{2,1,0:T(8,128)(2,1)} %broadcast_in_dim.111), calls=%async_computation | async-start | bytes 1310720 | tf_op jit(solution)/shard_map/all_to_all | solution.py:59
  30.2 8.2 %all_gather.15 = bf16[128,2048]{1,0:T(8,128)(2,1)S(1)} all-gather(bf16[128,512]{1,0:T(8,128)(2,1)} %param.15), channel_id=1, replica_groups=mesh['yl'=2,'c'=2,'yh'=2,'x'=4,'z'=8] {'yl','c'}, dimensions={1}, use_global_device_ids=true | all-gather | bytes 655360 | tf_op jit(solution)/shard_map/all_gather | solution.py:301
  39.0 10.1 %all-to-all-done = bf16[64,36,128]{2,1,0:T(8,128)(2,1)S(1)} async-done(((bf16[64,36,128]{2,1,0:T(8,128)(2,1)}), bf16[64,36,128]{2,1,0:T(8,128)(2,1)S(1)}, u32[]{:S(2)}, u32[]{:S(2)}) %all-to-all-start) | async-done | bytes 589856 | tf_op jit(solution)/shard_map/all_to_all | solution.py:59
  50.4 5.9 %all_gather.16 = f32[128,576]{0,1:T(8,128)S(1)} all-gather(f32[128,144]{0,1:T(8,128)S(1)} %pad_maximum_fusion.2), channel_id=1, replica_groups=mesh['yl'=2,'c'=2,'yh'=2,'x'=4,'z'=8] {'yl','c'}, dimensions={1}, use_global_device_ids=true | all-gather | bytes 368640 | tf_op jit(solution)/shard_map/all_gather | solution.py:316
  57.9 4.5 %all-to-all-start.1 = ((bf16[8,64,640]{2,1,0:T(8,128)(2,1)}), bf16[8,64,640]{2,1,0:T(8,128)(2,1)S(1)}, u32[]{:S(2)}, u32[]{:S(2)}) async-start(bf16[8,64,640]{2,1,0:T(8,128)(2,1)} %broadcast_in_dim.113), calls=%async_computation.1 | async-start | bytes 1310720 | tf_op jit(solution)/shard_map/all_to_all | solution.py:59
  62.7 19.3 %all-to-all-done.1 = bf16[8,64,640]{2,1,0:T(8,128)(2,1)S(1)} async-done(((bf16[8,64,640]{2,1,0:T(8,128)(2,1)}), bf16[8,64,640]{2,1,0:T(8,128)(2,1)S(1)}, u32[]{:S(2)}, u32[]{:S(2)}) %all-to-all-start.1) | async-done | bytes 655392 | tf_op jit(solution)/shard_map/all_to_all | solution.py:59
  84.4 2.0 collective-permute-start.5
  87.7 2.1 collective-permute-start.9
  89.8 12.0 %collective-permute-done.6 = bf16[1,256,640]{2,1,0:T(8,128)(2,1)S(1)} collective-permute-done((bf16[1,256,640]{2,1,0:T(8,128)(2,1)S(1)}, bf16[1,256,640]{2,1,0:T(8,128)(2,1)S(1)}, u32[]{:S(2)}, u32[]{:S(2)}) %collective-permute-start.6) | collective-permute-done | bytes 327712 | tf_op jit(solution)/shard_map/ppermute | solution.py:50
  104.1 2.6 collective-permute-start.10
  113.5 21.1 %collective-permute-done.10 = bf16[2,256,640]{2,1,0:T(8,128)(2,1)} collective-permute-done((bf16[2,256,640]{2,1,0:T(8,128)(2,1)S(1)}, bf16[2,256,640]{2,1,0:T(8,128)(2,1)}, u32[]{:S(2)}, u32[]{:S(2)}) %collective-permute-start.10) | collective-permute-done | bytes 655392 | tf_op jit(solution)/shard_map/ppermute | solution.py:50
  134.6 2.0 constant_dynamic-update-slice_fusion.14
  136.6 2.0 constant_dynamic-update-slice_fusion.13
  140.0 2.5 constant_dynamic-update-slice_fusion.7.a_own
  143.7 2.7 copy.75
  149.6 9.8 %shard_map.158.heads_ref = bf16[128,512]{1,0:T(8,128)(2,1)S(1)} custom-call(s32[19]{0:T(128)S(1)} %concatenate.52.meta, bf16[512,640]{1,0:T(8,128)(2,1)S(1)} %bitcast.103, s32[512,1]{1,0:T(8,128)S(1)} %copy.83.qlo_ref, s32[512,1]{1,0:T(8,128)S(1)} %copy.84.qpos_ref, bf16[8,256,640]{2,1,0:T(8,128)(2,1)} %constant_dynamic-update-slice_fusion.7.a_own, ...), custom_call_target="tpu_custom_call" | custom-call | flops 8999999488 | bytes 16000000 | tf_op jit(solution)/shard_map/pallas_call | solution.py:170
  159.4 15.2 %all-gather.7.cloned.1.call-done = bf16[2048,512]{1,0:T(8,128)(2,1)} async-done(((bf16[256,512]{1,0:T(8,128)(2,1)}), bf16[2048,512]{1,0:T(8,128)(2,1)}) %all-gather.7.cloned.1.call-update) | async-done | bytes 2097168 | tf_op jit(solution)/shard_map/all_gather | solution.py:343
  181.6 6.1 %collective-permute-done.15 = f32[128,512]{1,0:T(8,128)S(1)} collective-permute-done((f32[128,512]{1,0:T(8,128)S(1)}, f32[128,512]{1,0:T(8,128)S(1)}, u32[]{:S(2)}, u32[]{:S(2)}) %collective-permute-start.15) | collective-permute-done | bytes 262176 | tf_op jit(solution)/shard_map/ppermute | solution.py:54
  187.8 5.1 %all-gather.1 = f32[4,1,128]{2,1,0:T(1,128)S(1)} all-gather(f32[1,1,128]{2,1,0:T(1,128)S(1)} %bitcast.134), channel_id=2, replica_groups=mesh['yl'=2,'c'=2,'yh'=2,'x'=4,'z'=8] {'yl','c'}, dimensions={0}, use_global_device_ids=true | all-gather | bytes 2560 | tf_op jit(solution)/shard_map/all_gather | solution.py:426
  194.5 11.2 %all-to-all-start.2 = ((bf16[128,8,512]{2,1,0:T(8,128)(2,1)}), bf16[128,8,512]{2,1,0:T(8,128)(2,1)S(1)}, u32[]{:S(2)}, u32[]{:S(2)}) async-start(bf16[128,8,512]{2,1,0:T(8,128)(2,1)} %fusion.2), calls=%async_computation.2 | async-start | bytes 2097152 | tf_op jit(solution)/shard_map/all_to_all | solution.py:456
  205.7 2.0 collective-permute-start.17
  207.9 1.9 collective-permute-start.19
  209.8 25.1 %all-to-all-done.2 = bf16[128,8,512]{2,1,0:T(8,128)(2,1)S(1)} async-done(((bf16[128,8,512]{2,1,0:T(8,128)(2,1)}), bf16[128,8,512]{2,1,0:T(8,128)(2,1)S(1)}, u32[]{:S(2)}, u32[]{:S(2)}) %all-to-all-start.2) | async-done | bytes 1048608 | tf_op jit(solution)/shard_map/all_to_all | solution.py:456
  234.9 15.4 %collective-permute-done.17.wg1 = bf16[352,2048]{1,0:T(8,128)(2,1)} collective-permute-done((bf16[352,2048]{1,0:T(8,128)(2,1)S(1)}, bf16[352,2048]{1,0:T(8,128)(2,1)}, u32[]{:S(2)}, u32[]{:S(2)}) %collective-permute-start.17) | collective-permute-done | bytes 1441824 | tf_op jit(solution)/shard_map/ppermute | solution.py:54
  250.3 30.9 %collective-permute-done.18.wu1 = bf16[352,2048]{1,0:T(8,128)(2,1)} collective-permute-done((bf16[352,2048]{1,0:T(8,128)(2,1)}, bf16[352,2048]{1,0:T(8,128)(2,1)}, u32[]{:S(2)}, u32[]{:S(2)}) %collective-permute-start.18) | collective-permute-done | bytes 1441824 | tf_op jit(solution)/shard_map/ppermute | solution.py:54
  281.2 30.7 %collective-permute-done.19.wd1 = bf16[352,2048]{1,0:T(8,128)(2,1)} collective-permute-done((bf16[352,2048]{1,0:T(8,128)(2,1)}, bf16[352,2048]{1,0:T(8,128)(2,1)}, u32[]{:S(2)}, u32[]{:S(2)}) %collective-permute-start.19) | collective-permute-done | bytes 1441824 | tf_op jit(solution)/shard_map/ppermute | solution.py:54
  313.2 11.3 %shard_map.160 = (f32[2,512,512]{2,1,0:T(8,128)}, bf16[2,512,512]{2,1,0:T(8,128)(2,1)S(1)}) custom-call(s32[4]{0:T(128)S(1)} %pad_add_fusion.order, bf16[2,512,512]{2,1,0:T(8,128)(2,1)S(1)} %bitcast.102, bf16[2,512,512]{2,1,0:T(8,128)(2,1)S(1)} %collective-permute-done.16.oth_ref, bf16[352,2048]{1,0:T(8,128)(2,1)S(1)} %bitcast.105, ...), custom_call_target="tpu_custom_call" | custom-call | flops 4400000000 | bytes 14000000 | tf_op jit(solution)/shard_map/pallas_call | solution.py:237
  324.6 2.7 collective-permute-done.20
  327.2 2.9 add_convert_fusion
  330.2 13.1 %all-to-all-start.3 = ((bf16[128,8,512]{2,1,0:T(8,128)(2,1)}), bf16[128,8,512]{2,1,0:T(8,128)(2,1)S(1)}, u32[]{:S(2)}, u32[]{:S(2)}) async-start(bf16[128,8,512]{2,1,0:T(8,128)(2,1)} %bitcast.54), calls=%async_computation.3 | async-start | bytes 2097152 | tf_op jit(solution)/shard_map/all_to_all | solution.py:464
  350.6 21.6 %all-to-all-done.3 = bf16[128,8,512]{2,1,0:T(8,128)(2,1)S(1)} async-done(((bf16[128,8,512]{2,1,0:T(8,128)(2,1)}), bf16[128,8,512]{2,1,0:T(8,128)(2,1)S(1)}, u32[]{:S(2)}, u32[]{:S(2)}) %all-to-all-start.3) | async-done | bytes 1048608 | tf_op jit(solution)/shard_map/all_to_all | solution.py:464
  (158 shorter events, 41.1 us)
Async XLA Ops:
  7.2 31.8 %copy-start.4 = (bf16[32,768]{1,0:T(8,128)(2,1)S(1)}, bf16[32,768]{1,0:T(8,128)(2,1)}, u32[]{:S(2)}) copy-start(bf16[32,768]{1,0:T(8,128)(2,1)} %param.22) | copy-start | bytes 147460
  7.2 31.8 %copy-start.7 = (bf16[512,32]{0,1:T(8,128)(2,1)S(1)}, bf16[512,32]{0,1:T(8,128)(2,1)}, u32[]{:S(2)}) copy-start(bf16[512,32]{0,1:T(8,128)(2,1)} %param.25) | copy-start | bytes 98308
  7.2 31.8 %copy-start.8 = (bf16[8,1024]{1,0:T(8,128)(2,1)S(1)}, bf16[8,1024]{1,0:T(8,128)(2,1)}, u32[]{:S(2)}) copy-start(bf16[8,1024]{1,0:T(8,128)(2,1)} %param.24) | copy-start | bytes 49156
  8.1 30.9 %collective-permute-start.2 = (bf16[1,32,1536]{2,1,0:T(8,128)(2,1)S(1)}, bf16[1,32,1536]{2,1,0:T(8,128)(2,1)S(1)}, u32[]{:S(2)}, u32[]{:S(2)}) collective-permute-start(bf16[1,32,1536]{2,1,0:T(8,128)(2,1)S(1)} %maximum_bitcast_fusion), channel_id=1, source_target_pairs={{0,8},{8,16},{16,24},{24,0},{1,9},{9,17},{17,25},{25,1},{2,10},{10... | collective-permute-start | bytes 294920 | tf_op jit(solution)/shard_map/ppermute | solution.py:50
  8.6 30.3 %collective-permute-start.1 = (bf16[1,32,1536]{2,1,0:T(8,128)(2,1)S(1)}, bf16[1,32,1536]{2,1,0:T(8,128)(2,1)S(1)}, u32[]{:S(2)}, u32[]{:S(2)}) collective-permute-start(bf16[1,32,1536]{2,1,0:T(8,128)(2,1)S(1)} %maximum_bitcast_fusion), channel_id=1, source_target_pairs={{0,16},{8,24},{16,0},{24,8},{1,17},{9,25},{17,1},{25,9},{2,18},{10... | collective-permute-start | bytes 294920 | tf_op jit(solution)/shard_map/ppermute | solution.py:50
  11.0 27.9 %collective-permute-start = (bf16[1,32,1536]{2,1,0:T(8,128)(2,1)S(1)}, bf16[1,32,1536]{2,1,0:T(8,128)(2,1)S(1)}, u32[]{:S(2)}, u32[]{:S(2)}) collective-permute-start(bf16[1,32,1536]{2,1,0:T(8,128)(2,1)S(1)} %maximum_bitcast_fusion), channel_id=1, source_target_pairs={{0,24},{8,0},{16,8},{24,16},{1,25},{9,1},{17,9},{25,17},{2,26},{10... | collective-permute-start | bytes 294920 | tf_op jit(solution)/shard_map/ppermute | solution.py:50
  13.4 36.2 %copy-start.10 = (f32[2048]{0:T(1024)S(1)}, f32[2048]{0:T(1024)}, u32[]{:S(2)}) copy-start(f32[2048]{0:T(1024)} %param.19) | copy-start | bytes 24580
  13.4 35.7 %all-to-all-start = ((bf16[64,36,128]{2,1,0:T(8,128)(2,1)}), bf16[64,36,128]{2,1,0:T(8,128)(2,1)S(1)}, u32[]{:S(2)}, u32[]{:S(2)}) async-start(bf16[64,36,128]{2,1,0:T(8,128)(2,1)} %broadcast_in_dim.111), calls=%async_computation | async-start | bytes 1310720 | tf_op jit(solution)/shard_map/all_to_all | solution.py:59
  57.9 24.1 %all-to-all-start.1 = ((bf16[8,64,640]{2,1,0:T(8,128)(2,1)}), bf16[8,64,640]{2,1,0:T(8,128)(2,1)S(1)}, u32[]{:S(2)}, u32[]{:S(2)}) async-start(bf16[8,64,640]{2,1,0:T(8,128)(2,1)} %broadcast_in_dim.113), calls=%async_computation.1 | async-start | bytes 1310720 | tf_op jit(solution)/shard_map/all_to_all | solution.py:59
  62.4 81.3 %all-gather.5.cloned.1.call-start = ((), (), s32[]{:S(2)}) async-start(), calls=%async_computation.4 | async-start | bytes 4718592 | tf_op jit(solution)/shard_map/all_gather | solution.py:335
  62.5 20.7 %collective-permute-start.3 = (bf16[4,32,1536]{2,1,0:T(8,128)(2,1)S(1)}, bf16[4,32,1536]{2,1,0:T(8,128)(2,1)S(1)}, u32[]{:S(2)}, u32[]{:S(2)}) collective-permute-start(bf16[4,32,1536]{2,1,0:T(8,128)(2,1)S(1)} %constant_dynamic-slice_fusion), channel_id=1, source_target_pairs={{0,32},{32,0},{1,33},{33,1},{2,34},{34,2},{3,35},{35,3},{4,36},{36... | collective-permute-start | bytes 1179656 | tf_op jit(solution)/shard_map/ppermute | solution.py:54
  84.2 90.4 %all-gather.7.cloned.1.call-start = ((), (), s32[]{:S(2)}) async-start(), calls=%async_computation.5 | async-start | bytes 2359296 | tf_op jit(solution)/shard_map/all_gather | solution.py:343
  84.4 17.4 %collective-permute-start.6 = (bf16[1,256,640]{2,1,0:T(8,128)(2,1)S(1)}, bf16[1,256,640]{2,1,0:T(8,128)(2,1)S(1)}, u32[]{:S(2)}, u32[]{:S(2)}) collective-permute-start(bf16[1,256,640]{2,1,0:T(8,128)(2,1)S(1)} %bitcast.117), channel_id=1, source_target_pairs={{0,24},{8,0},{16,8},{24,16},{1,25},{9,1},{17,9},{25,17},{2,26},{10... | collective-permute-start | bytes 983048 | tf_op jit(solution)/shard_map/ppermute | solution.py:50
  84.4 17.3 %collective-permute-start.5 = (bf16[1,256,640]{2,1,0:T(8,128)(2,1)S(1)}, bf16[1,256,640]{2,1,0:T(8,128)(2,1)S(1)}, u32[]{:S(2)}, u32[]{:S(2)}) collective-permute-start(bf16[1,256,640]{2,1,0:T(8,128)(2,1)S(1)} %bitcast.118), channel_id=1, source_target_pairs={{0,16},{8,24},{16,0},{24,8},{1,17},{9,25},{17,1},{25,9},{2,18},{10... | collective-permute-start | bytes 983048 | tf_op jit(solution)/shard_map/ppermute | solution.py:50
  86.4 16.0 %collective-permute-start.4 = (bf16[1,256,640]{2,1,0:T(8,128)(2,1)S(1)}, bf16[1,256,640]{2,1,0:T(8,128)(2,1)S(1)}, u32[]{:S(2)}, u32[]{:S(2)}) collective-permute-start(bf16[1,256,640]{2,1,0:T(8,128)(2,1)S(1)} %bitcast.119), channel_id=1, source_target_pairs={{0,8},{8,16},{16,24},{24,0},{1,9},{9,17},{17,25},{25,1},{2,10},{10... | collective-permute-start | bytes 983048 | tf_op jit(solution)/shard_map/ppermute | solution.py:50
  87.7 16.3 %collective-permute-start.9 = (bf16[1,256,640]{2,1,0:T(8,128)(2,1)S(1)}, bf16[1,256,640]{2,1,0:T(8,128)(2,1)S(1)}, u32[]{:S(2)}, u32[]{:S(2)}) collective-permute-start(bf16[1,256,640]{2,1,0:T(8,128)(2,1)S(1)} %bitcast.114), channel_id=1, source_target_pairs={{0,32},{32,0},{1,33},{33,1},{2,34},{34,2},{3,35},{35,3},{4,36},{36... | collective-permute-start | bytes 983048 | tf_op jit(solution)/shard_map/ppermute | solution.py:54
  103.7 36.3 %collective-permute-start.7 = (bf16[4,256,640]{2,1,0:T(8,128)(2,1)}, bf16[4,256,640]{2,1,0:T(8,128)(2,1)}, u32[]{:S(2)}, u32[]{:S(2)}) collective-permute-start(bf16[4,256,640]{2,1,0:T(8,128)(2,1)} %pad_maximum_fusion), channel_id=1, source_target_pairs={{0,32},{32,0},{1,33},{33,1},{2,34},{34,2},{3,35},{35,3},{4,36},{36... | collective-permute-start | bytes 3932168 | tf_op jit(solution)/shard_map/ppermute | solution.py:54
  104.1 30.6 %collective-permute-start.10 = (bf16[2,256,640]{2,1,0:T(8,128)(2,1)S(1)}, bf16[2,256,640]{2,1,0:T(8,128)(2,1)}, u32[]{:S(2)}, u32[]{:S(2)}) collective-permute-start(bf16[2,256,640]{2,1,0:T(8,128)(2,1)S(1)} %pad_maximum_fusion.1), channel_id=1, source_target_pairs={{0,8},{8,16},{16,24},{24,0},{1,9},{9,17},{17,25},{25,1},{2,10},{10... | collective-permute-start | bytes 1966088 | tf_op jit(solution)/shard_map/ppermute | solution.py:50
  107.4 29.2 %collective-permute-start.11 = (bf16[2,256,640]{2,1,0:T(8,128)(2,1)S(1)}, bf16[2,256,640]{2,1,0:T(8,128)(2,1)}, u32[]{:S(2)}, u32[]{:S(2)}) collective-permute-start(bf16[2,256,640]{2,1,0:T(8,128)(2,1)S(1)} %pad_maximum_fusion.1), channel_id=1, source_target_pairs={{0,16},{8,24},{16,0},{24,8},{1,17},{9,25},{17,1},{25,9},{2,18},{10... | collective-permute-start | bytes 1966088 | tf_op jit(solution)/shard_map/ppermute | solution.py:50
  110.1 29.0 %collective-permute-start.12 = (bf16[2,256,640]{2,1,0:T(8,128)(2,1)S(1)}, bf16[2,256,640]{2,1,0:T(8,128)(2,1)S(1)}, u32[]{:S(2)}, u32[]{:S(2)}) collective-permute-start(bf16[2,256,640]{2,1,0:T(8,128)(2,1)S(1)} %pad_maximum_fusion.1), channel_id=1, source_target_pairs={{0,24},{8,0},{16,8},{24,16},{1,25},{9,1},{17,9},{25,17},{2,26},{10... | collective-permute-start | bytes 1966088 | tf_op jit(solution)/shard_map/ppermute | solution.py:50
  140.0 9.6 %collective-permute-start.13 = (bf16[8,256,640]{2,1,0:T(8,128)(2,1)}, bf16[8,256,640]{2,1,0:T(8,128)(2,1)}, u32[]{:S(2)}, u32[]{:S(2)}) collective-permute-start(bf16[8,256,640]{2,1,0:T(8,128)(2,1)} %constant_dynamic-update-slice_fusion.12.b_own), channel_id=1, source_target_pairs={{0,64},{64,0},{1,65},{65,1},{2,66},{66,2},{3,67},{67,3},{4,68},{68... | collective-permute-start | bytes 7864328 | tf_op jit(solution)/shard_map/ppermute | solution.py:54
  142.5 7.1 %collective-permute-start.8 = (bf16[8,256,640]{2,1,0:T(8,128)(2,1)}, bf16[8,256,640]{2,1,0:T(8,128)(2,1)}, u32[]{:S(2)}, u32[]{:S(2)}) collective-permute-start(bf16[8,256,640]{2,1,0:T(8,128)(2,1)} %constant_dynamic-update-slice_fusion.7.a_own), channel_id=1, source_target_pairs={{0,64},{64,0},{1,65},{65,1},{2,66},{66,2},{3,67},{67,3},{4,68},{68... | collective-permute-start | bytes 7864328 | tf_op jit(solution)/shard_map/ppermute | solution.py:54
  177.1 2.0 collective-permute-start.14
  179.2 26.5 %copy-start.1 = (bf16[1,2048,352]{1,2,0:T(8,128)(2,1)S(1)}, bf16[1,2048,352]{1,2,0:T(8,128)(2,1)}, u32[]{:S(2)}) copy-start(bf16[1,2048,352]{1,2,0:T(8,128)(2,1)} %param.26) | copy-start | bytes 4325380
  179.3 8.4 %collective-permute-start.15 = (f32[128,512]{1,0:T(8,128)S(1)}, f32[128,512]{1,0:T(8,128)S(1)}, u32[]{:S(2)}, u32[]{:S(2)}) collective-permute-start(f32[128,512]{1,0:T(8,128)S(1)} %dynamic-slice_bitcast_fusion.1), channel_id=1, source_target_pairs={{0,128},{128,0},{1,129},{129,1},{2,130},{130,2},{3,131},{131,3},{4... | collective-permute-start | bytes 786440 | tf_op jit(solution)/shard_map/ppermute | solution.py:54
  194.5 40.3 %all-to-all-start.2 = ((bf16[128,8,512]{2,1,0:T(8,128)(2,1)}), bf16[128,8,512]{2,1,0:T(8,128)(2,1)S(1)}, u32[]{:S(2)}, u32[]{:S(2)}) async-start(bf16[128,8,512]{2,1,0:T(8,128)(2,1)} %fusion.2), calls=%async_computation.2 | async-start | bytes 2097152 | tf_op jit(solution)/shard_map/all_to_all | solution.py:456
  205.7 44.6 %collective-permute-start.17 = (bf16[352,2048]{1,0:T(8,128)(2,1)S(1)}, bf16[352,2048]{1,0:T(8,128)(2,1)}, u32[]{:S(2)}, u32[]{:S(2)}) collective-permute-start(bf16[352,2048]{1,0:T(8,128)(2,1)S(1)} %bitcast.104), channel_id=1, source_target_pairs={{0,128},{128,0},{1,129},{129,1},{2,130},{130,2},{3,131},{131,3},{4... | collective-permute-start | bytes 4325384 | tf_op jit(solution)/shard_map/ppermute | solution.py:54
  207.7 73.5 %collective-permute-start.18 = (bf16[352,2048]{1,0:T(8,128)(2,1)}, bf16[352,2048]{1,0:T(8,128)(2,1)}, u32[]{:S(2)}, u32[]{:S(2)}) collective-permute-start(bf16[352,2048]{1,0:T(8,128)(2,1)} %bitcast.106), channel_id=1, source_target_pairs={{0,128},{128,0},{1,129},{129,1},{2,130},{130,2},{3,131},{131,3},{4... | collective-permute-start | bytes 4325384 | tf_op jit(solution)/shard_map/ppermute | solution.py:54
  207.9 104.0 %collective-permute-start.19 = (bf16[352,2048]{1,0:T(8,128)(2,1)}, bf16[352,2048]{1,0:T(8,128)(2,1)}, u32[]{:S(2)}, u32[]{:S(2)}) collective-permute-start(bf16[352,2048]{1,0:T(8,128)(2,1)} %bitcast.135), channel_id=1, source_target_pairs={{0,128},{128,0},{1,129},{129,1},{2,130},{130,2},{3,131},{131,3},{4... | collective-permute-start | bytes 4325384 | tf_op jit(solution)/shard_map/ppermute | solution.py:54
  234.8 77.1 %collective-permute-start.16 = (bf16[2,512,512]{2,1,0:T(8,128)(2,1)S(1)}, bf16[2,512,512]{2,1,0:T(8,128)(2,1)S(1)}, u32[]{:S(2)}, u32[]{:S(2)}) collective-permute-start(bf16[2,512,512]{2,1,0:T(8,128)(2,1)S(1)} %bitcast.101), channel_id=1, source_target_pairs={{0,64},{64,0},{1,65},{65,1},{2,66},{66,2},{3,67},{67,3},{4,68},{68... | collective-permute-start | bytes 3145736 | tf_op jit(solution)/shard_map/ppermute | solution.py:54
  324.6 2.7 collective-permute-start.20
  330.2 42.0 %all-to-all-start.3 = ((bf16[128,8,512]{2,1,0:T(8,128)(2,1)}), bf16[128,8,512]{2,1,0:T(8,128)(2,1)S(1)}, u32[]{:S(2)}, u32[]{:S(2)}) async-start(bf16[128,8,512]{2,1,0:T(8,128)(2,1)} %bitcast.54), calls=%async_computation.3 | async-start | bytes 2097152 | tf_op jit(solution)/shard_map/all_to_all | solution.py:464
  (12 other events, 118.0 us)
Sparse Core Ops, SparseCore 0:
  84.4 47.4 all-gather.4
  133.6 40.9 all-gather.6
where the time goes:
time: 385 us; the launch traced here: 381 us
  waiting for transfers between devices  213 us (55%)
  starting transfers between devices  62.6 us (16%)
  local copies, waits for them, and re-layouts  27.6 us (7%)
  Pallas kernels  22 us (6%)
  between operations  20.4 us (5%)
  blocking collectives  19.1 us (5%)
  other arithmetic  9.95 us (3%)
  matrix products  5.82 us (2%)
    ppermute x12, waiting for transfers between devices, swap(): return lax.ppermute(values, axis, SWAP)  87.4 us
    ppermute x9, waiting for transfers between devices, shift(): lax.ppermute(values, axis, [(i, (i + step) % size) for i in range(size)])  34.2 us
    all_to_all x2, waiting for transfers between devices, spread(): return lax.all_to_all(blocks, axis, split_axis=0, concat_axis=0, tiled=True)  29.5 us
    all_to_all x1, waiting for transfers between devices, layer(): lax.all_to_all(outgoing.reshape(YL * GROUPS, chunk, share), ('yl',) + GY,...  25.1 us
    all_to_all x1, waiting for transfers between devices, layer(): lax.all_to_all(summed.reshape(YL * GROUPS, chunk, share), ('yl',) + GY, s...  21.6 us
    all_to_all x2, starting transfers between devices, spread(): return lax.all_to_all(blocks, axis, split_axis=0, concat_axis=0, tiled=True)  19.1 us
    all_gather x1, waiting for transfers between devices, layer(): lax.all_gather(near_weights[:, :, front_cols:].reshape(crowd * depth, lat...  15.2 us
    all_to_all x1, starting transfers between devices, layer(): lax.all_to_all(summed.reshape(YL * GROUPS, chunk, share), ('yl',) + GY, s...  13.1 us
  transfers between devices with their start and end apart: 27, of which 15 were waited for; matrix products, arithmetic and copies ran while one was open for 8% of the time, Pallas kernels for 3%

commit v1 on v0

--- a/solution.py
+++ b/solution.py
@@ -347,9 +347,11 @@
     quarter = half // 2
     a0 = along_z[:, :quarter].reshape(1, ZS * quarter, WIDE)
     b0 = along_z[:, quarter:].reshape(1, ZS * quarter, WIDE)
-    b1 = jnp.concatenate([b0, swap(b0, "yh")], axis=0)
+    b0_far = swap(b0, "yh")
+    b1 = jnp.concatenate([b0, b0_far], axis=0)
     a1 = jnp.concatenate([a0] + [shift(a0, "x", XS, k) for k in range(1, XS)], axis=0)
-    a_own = jnp.concatenate([a1, swap(a1, "yh")], axis=0)
+    a1_far = swap(a1, "yh")
+    a_own = jnp.concatenate([a1, a1_far], axis=0)
     b_own = jnp.concatenate([b1] + [shift(b1, "x", XS, k) for k in range(1, XS)], axis=0)
     a_oth = swap(a_own, "c")
     b_oth = swap(b_own, "c")
@@ -456,7 +458,8 @@
     incoming = lax.all_to_all(
         outgoing.reshape(YL * GROUPS, chunk, share), ("yl",) + GY,
         split_axis=0, concat_axis=0, tiled=True,
-    ).reshape(YL, group_rows, share)
+    )
+    incoming = incoming.reshape(YL, group_rows, share)
     kept, given = experts(
         order, incoming, swap(incoming, "c"), gate_t, up_t, down, gate_far, up_far, down_far
     )

time: 385 us -> 385 us (level)
  no operation moved by 1% of the time
where the time goes in v1:
time: 385 us; the launch traced here: 381 us
  waiting for transfers between devices  213 us (55%)
  starting transfers between devices  62.6 us (16%)
  local copies, waits for them, and re-layouts  27.6 us (7%)
  Pallas kernels  22 us (6%)
  between operations  20.4 us (5%)
  blocking collectives  19.1 us (5%)
  other arithmetic  9.95 us (3%)
  matrix products  5.82 us (2%)
    ppermute x12, waiting for transfers between devices, swap(): return lax.ppermute(values, axis, SWAP)  87.4 us
    ppermute x9, waiting for transfers between devices, shift(): lax.ppermute(values, axis, [(i, (i + step) % size) for i in range(size)])  34.2 us
    all_to_all x2, waiting for transfers between devices, spread(): return lax.all_to_all(blocks, axis, split_axis=0, concat_axis=0, tiled=True)  29.5 us
    all_to_all x1, waiting for transfers between devices, layer(): lax.all_to_all(outgoing.reshape(YL * GROUPS, chunk, share), ('yl',) + GY,...  25.1 us
    all_to_all x1, waiting for transfers between devices, layer(): lax.all_to_all(summed.reshape(YL * GROUPS, chunk, share), ('yl',) + GY, s...  21.6 us
    all_to_all x2, starting transfers between devices, spread(): return lax.all_to_all(blocks, axis, split_axis=0, concat_axis=0, tiled=True)  19.1 us
    all_gather x1, waiting for transfers between devices, layer(): lax.all_gather(near_weights[:, :, front_cols:].reshape(crowd * depth, lat...  15.2 us
    all_to_all x1, starting transfers between devices, layer(): lax.all_to_all(summed.reshape(YL * GROUPS, chunk, share), ('yl',) + GY, s...  13.1 us
  transfers between devices with their start and end apart: 27, of which 15 were waited for; matrix products, arithmetic and copies ran while one was open for 8% of the time, Pallas kernels for 3%

profile of v1, /device:TPU:38, one launch (start us, length us, event | category | flops | bytes accessed | tf_op | source)
XLA Modules:
  0.0 380.7 jit_solution(6229039472847465605)
XLA Ops:
  8.6 2.4 collective-permute-start.1
  13.4 14.6 %all-to-all-start = ((bf16[64,36,128]{2,1,0:T(8,128)(2,1)}), bf16[64,36,128]{2,1,0:T(8,128)(2,1)S(1)}, u32[]{:S(2)}, u32[]{:S(2)}) async-start(bf16[64,36,128]{2,1,0:T(8,128)(2,1)} %broadcast_in_dim.111), calls=%async_computation | async-start | bytes 1310720 | tf_op jit(solution)/shard_map/all_to_all | solution.py:59
  30.2 8.2 %all_gather.15 = bf16[128,2048]{1,0:T(8,128)(2,1)S(1)} all-gather(bf16[128,512]{1,0:T(8,128)(2,1)} %param.15), channel_id=1, replica_groups=mesh['yl'=2,'c'=2,'yh'=2,'x'=4,'z'=8] {'yl','c'}, dimensions={1}, use_global_device_ids=true | all-gather | bytes 655360 | tf_op jit(solution)/shard_map/all_gather | solution.py:301
  39.0 10.1 %all-to-all-done = bf16[64,36,128]{2,1,0:T(8,128)(2,1)S(1)} async-done(((bf16[64,36,128]{2,1,0:T(8,128)(2,1)}), bf16[64,36,128]{2,1,0:T(8,128)(2,1)S(1)}, u32[]{:S(2)}, u32[]{:S(2)}) %all-to-all-start) | async-done | bytes 589856 | tf_op jit(solution)/shard_map/all_to_all | solution.py:59
  50.4 5.9 %all_gather.16 = f32[128,576]{0,1:T(8,128)S(1)} all-gather(f32[128,144]{0,1:T(8,128)S(1)} %pad_maximum_fusion.2), channel_id=1, replica_groups=mesh['yl'=2,'c'=2,'yh'=2,'x'=4,'z'=8] {'yl','c'}, dimensions={1}, use_global_device_ids=true | all-gather | bytes 368640 | tf_op jit(solution)/shard_map/all_gather | solution.py:316
  57.9 4.5 %all-to-all-start.1 = ((bf16[8,64,640]{2,1,0:T(8,128)(2,1)}), bf16[8,64,640]{2,1,0:T(8,128)(2,1)S(1)}, u32[]{:S(2)}, u32[]{:S(2)}) async-start(bf16[8,64,640]{2,1,0:T(8,128)(2,1)} %broadcast_in_dim.113), calls=%async_computation.1 | async-start | bytes 1310720 | tf_op jit(solution)/shard_map/all_to_all | solution.py:59
  62.7 19.3 %all-to-all-done.1 = bf16[8,64,640]{2,1,0:T(8,128)(2,1)S(1)} async-done(((bf16[8,64,640]{2,1,0:T(8,128)(2,1)}), bf16[8,64,640]{2,1,0:T(8,128)(2,1)S(1)}, u32[]{:S(2)}, u32[]{:S(2)}) %all-to-all-start.1) | async-done | bytes 655392 | tf_op jit(solution)/shard_map/all_to_all | solution.py:59
  84.4 2.0 collective-permute-start.5
  87.7 2.1 collective-permute-start.9
  89.8 12.0 %collective-permute-done.6 = bf16[1,256,640]{2,1,0:T(8,128)(2,1)S(1)} collective-permute-done((bf16[1,256,640]{2,1,0:T(8,128)(2,1)S(1)}, bf16[1,256,640]{2,1,0:T(8,128)(2,1)S(1)}, u32[]{:S(2)}, u32[]{:S(2)}) %collective-permute-start.6) | collective-permute-done | bytes 327712 | tf_op jit(solution)/shard_map/ppermute | solution.py:50
  104.1 2.6 collective-permute-start.10
  113.5 21.1 %collective-permute-done.10 = bf16[2,256,640]{2,1,0:T(8,128)(2,1)} collective-permute-done((bf16[2,256,640]{2,1,0:T(8,128)(2,1)S(1)}, bf16[2,256,640]{2,1,0:T(8,128)(2,1)}, u32[]{:S(2)}, u32[]{:S(2)}) %collective-permute-start.10) | collective-permute-done | bytes 655392 | tf_op jit(solution)/shard_map/ppermute | solution.py:50
  134.6 2.0 constant_dynamic-update-slice_fusion.14
  136.6 2.0 constant_dynamic-update-slice_fusion.13
  140.0 2.5 constant_dynamic-update-slice_fusion.7.a_own
  143.7 2.7 copy.75
  149.6 9.8 %shard_map.158.heads_ref = bf16[128,512]{1,0:T(8,128)(2,1)S(1)} custom-call(s32[19]{0:T(128)S(1)} %concatenate.52.meta, bf16[512,640]{1,0:T(8,128)(2,1)S(1)} %bitcast.103, s32[512,1]{1,0:T(8,128)S(1)} %copy.83.qlo_ref, s32[512,1]{1,0:T(8,128)S(1)} %copy.84.qpos_ref, bf16[8,256,640]{2,1,0:T(8,128)(2,1)} %constant_dynamic-update-slice_fusion.7.a_own, ...), custom_call_target="tpu_custom_call" | custom-call | flops 8999999488 | bytes 16000000 | tf_op jit(solution)/shard_map/pallas_call | solution.py:170
  159.4 15.2 %all-gather.7.cloned.1.call-done = bf16[2048,512]{1,0:T(8,128)(2,1)} async-done(((bf16[256,512]{1,0:T(8,128)(2,1)}), bf16[2048,512]{1,0:T(8,128)(2,1)}) %all-gather.7.cloned.1.call-update) | async-done | bytes 2097168 | tf_op jit(solution)/shard_map/all_gather | solution.py:343
  181.6 6.1 %collective-permute-done.15 = f32[128,512]{1,0:T(8,128)S(1)} collective-permute-done((f32[128,512]{1,0:T(8,128)S(1)}, f32[128,512]{1,0:T(8,128)S(1)}, u32[]{:S(2)}, u32[]{:S(2)}) %collective-permute-start.15) | collective-permute-done | bytes 262176 | tf_op jit(solution)/shard_map/ppermute | solution.py:54
  187.8 5.1 %all-gather.1 = f32[4,1,128]{2,1,0:T(1,128)S(1)} all-gather(f32[1,1,128]{2,1,0:T(1,128)S(1)} %bitcast.134), channel_id=2, replica_groups=mesh['yl'=2,'c'=2,'yh'=2,'x'=4,'z'=8] {'yl','c'}, dimensions={0}, use_global_device_ids=true | all-gather | bytes 2560 | tf_op jit(solution)/shard_map/all_gather | solution.py:428
  194.5 11.2 %all-to-all-start.2 = ((bf16[128,8,512]{2,1,0:T(8,128)(2,1)}), bf16[128,8,512]{2,1,0:T(8,128)(2,1)S(1)}, u32[]{:S(2)}, u32[]{:S(2)}) async-start(bf16[128,8,512]{2,1,0:T(8,128)(2,1)} %fusion.2), calls=%async_computation.2 | async-start | bytes 2097152 | tf_op jit(solution)/shard_map/all_to_all | solution.py:458
  205.7 2.0 collective-permute-start.17
  207.9 1.9 collective-permute-start.19
  209.8 25.1 %all-to-all-done.2 = bf16[128,8,512]{2,1,0:T(8,128)(2,1)S(1)} async-done(((bf16[128,8,512]{2,1,0:T(8,128)(2,1)}), bf16[128,8,512]{2,1,0:T(8,128)(2,1)S(1)}, u32[]{:S(2)}, u32[]{:S(2)}) %all-to-all-start.2) | async-done | bytes 1048608 | tf_op jit(solution)/shard_map/all_to_all | solution.py:458
  234.9 15.4 %collective-permute-done.17.wg1 = bf16[352,2048]{1,0:T(8,128)(2,1)} collective-permute-done((bf16[352,2048]{1,0:T(8,128)(2,1)S(1)}, bf16[352,2048]{1,0:T(8,128)(2,1)}, u32[]{:S(2)}, u32[]{:S(2)}) %collective-permute-start.17) | collective-permute-done | bytes 1441824 | tf_op jit(solution)/shard_map/ppermute | solution.py:54
  250.3 30.9 %collective-permute-done.18.wu1 = bf16[352,2048]{1,0:T(8,128)(2,1)} collective-permute-done((bf16[352,2048]{1,0:T(8,128)(2,1)}, bf16[352,2048]{1,0:T(8,128)(2,1)}, u32[]{:S(2)}, u32[]{:S(2)}) %collective-permute-start.18) | collective-permute-done | bytes 1441824 | tf_op jit(solution)/shard_map/ppermute | solution.py:54
  281.2 30.7 %collective-permute-done.19.wd1 = bf16[352,2048]{1,0:T(8,128)(2,1)} collective-permute-done((bf16[352,2048]{1,0:T(8,128)(2,1)}, bf16[352,2048]{1,0:T(8,128)(2,1)}, u32[]{:S(2)}, u32[]{:S(2)}) %collective-permute-start.19) | collective-permute-done | bytes 1441824 | tf_op jit(solution)/shard_map/ppermute | solution.py:54
  313.2 11.3 %shard_map.160 = (f32[2,512,512]{2,1,0:T(8,128)}, bf16[2,512,512]{2,1,0:T(8,128)(2,1)S(1)}) custom-call(s32[4]{0:T(128)S(1)} %pad_add_fusion.order, bf16[2,512,512]{2,1,0:T(8,128)(2,1)S(1)} %bitcast.102, bf16[2,512,512]{2,1,0:T(8,128)(2,1)S(1)} %collective-permute-done.16.oth_ref, bf16[352,2048]{1,0:T(8,128)(2,1)S(1)} %bitcast.105, ...), custom_call_target="tpu_custom_call" | custom-call | flops 4400000000 | bytes 14000000 | tf_op jit(solution)/shard_map/pallas_call | solution.py:237
  324.6 2.7 collective-permute-done.20
  327.2 2.9 add_convert_fusion
  330.2 13.1 %all-to-all-start.3 = ((bf16[128,8,512]{2,1,0:T(8,128)(2,1)}), bf16[128,8,512]{2,1,0:T(8,128)(2,1)S(1)}, u32[]{:S(2)}, u32[]{:S(2)}) async-start(bf16[128,8,512]{2,1,0:T(8,128)(2,1)} %bitcast.54), calls=%async_computation.3 | async-start | bytes 2097152 | tf_op jit(solution)/shard_map/all_to_all | solution.py:467
  350.6 21.6 %all-to-all-done.3 = bf16[128,8,512]{2,1,0:T(8,128)(2,1)S(1)} async-done(((bf16[128,8,512]{2,1,0:T(8,128)(2,1)}), bf16[128,8,512]{2,1,0:T(8,128)(2,1)S(1)}, u32[]{:S(2)}, u32[]{:S(2)}) %all-to-all-start.3) | async-done | bytes 1048608 | tf_op jit(solution)/shard_map/all_to_all | solution.py:467
  (158 shorter events, 41.1 us)
Async XLA Ops:
  7.2 31.8 %copy-start.4 = (bf16[32,768]{1,0:T(8,128)(2,1)S(1)}, bf16[32,768]{1,0:T(8,128)(2,1)}, u32[]{:S(2)}) copy-start(bf16[32,768]{1,0:T(8,128)(2,1)} %param.22) | copy-start | bytes 147460
  7.2 31.8 %copy-start.7 = (bf16[512,32]{0,1:T(8,128)(2,1)S(1)}, bf16[512,32]{0,1:T(8,128)(2,1)}, u32[]{:S(2)}) copy-start(bf16[512,32]{0,1:T(8,128)(2,1)} %param.25) | copy-start | bytes 98308
  7.2 31.8 %copy-start.8 = (bf16[8,1024]{1,0:T(8,128)(2,1)S(1)}, bf16[8,1024]{1,0:T(8,128)(2,1)}, u32[]{:S(2)}) copy-start(bf16[8,1024]{1,0:T(8,128)(2,1)} %param.24) | copy-start | bytes 49156
  8.1 30.9 %collective-permute-start.2 = (bf16[1,32,1536]{2,1,0:T(8,128)(2,1)S(1)}, bf16[1,32,1536]{2,1,0:T(8,128)(2,1)S(1)}, u32[]{:S(2)}, u32[]{:S(2)}) collective-permute-start(bf16[1,32,1536]{2,1,0:T(8,128)(2,1)S(1)} %maximum_bitcast_fusion), channel_id=1, source_target_pairs={{0,8},{8,16},{16,24},{24,0},{1,9},{9,17},{17,25},{25,1},{2,10},{10... | collective-permute-start | bytes 294920 | tf_op jit(solution)/shard_map/ppermute | solution.py:50
  8.6 30.3 %collective-permute-start.1 = (bf16[1,32,1536]{2,1,0:T(8,128)(2,1)S(1)}, bf16[1,32,1536]{2,1,0:T(8,128)(2,1)S(1)}, u32[]{:S(2)}, u32[]{:S(2)}) collective-permute-start(bf16[1,32,1536]{2,1,0:T(8,128)(2,1)S(1)} %maximum_bitcast_fusion), channel_id=1, source_target_pairs={{0,16},{8,24},{16,0},{24,8},{1,17},{9,25},{17,1},{25,9},{2,18},{10... | collective-permute-start | bytes 294920 | tf_op jit(solution)/shard_map/ppermute | solution.py:50
  11.0 27.9 %collective-permute-start = (bf16[1,32,1536]{2,1,0:T(8,128)(2,1)S(1)}, bf16[1,32,1536]{2,1,0:T(8,128)(2,1)S(1)}, u32[]{:S(2)}, u32[]{:S(2)}) collective-permute-start(bf16[1,32,1536]{2,1,0:T(8,128)(2,1)S(1)} %maximum_bitcast_fusion), channel_id=1, source_target_pairs={{0,24},{8,0},{16,8},{24,16},{1,25},{9,1},{17,9},{25,17},{2,26},{10... | collective-permute-start | bytes 294920 | tf_op jit(solution)/shard_map/ppermute | solution.py:50
  13.4 36.2 %copy-start.10 = (f32[2048]{0:T(1024)S(1)}, f32[2048]{0:T(1024)}, u32[]{:S(2)}) copy-start(f32[2048]{0:T(1024)} %param.19) | copy-start | bytes 24580
  13.4 35.7 %all-to-all-start = ((bf16[64,36,128]{2,1,0:T(8,128)(2,1)}), bf16[64,36,128]{2,1,0:T(8,128)(2,1)S(1)}, u32[]{:S(2)}, u32[]{:S(2)}) async-start(bf16[64,36,128]{2,1,0:T(8,128)(2,1)} %broadcast_in_dim.111), calls=%async_computation | async-start | bytes 1310720 | tf_op jit(solution)/shard_map/all_to_all | solution.py:59
  57.9 24.1 %all-to-all-start.1 = ((bf16[8,64,640]{2,1,0:T(8,128)(2,1)}), bf16[8,64,640]{2,1,0:T(8,128)(2,1)S(1)}, u32[]{:S(2)}, u32[]{:S(2)}) async-start(bf16[8,64,640]{2,1,0:T(8,128)(2,1)} %broadcast_in_dim.113), calls=%async_computation.1 | async-start | bytes 1310720 | tf_op jit(solution)/shard_map/all_to_all | solution.py:59
  62.4 81.3 %all-gather.5.cloned.1.call-start = ((), (), s32[]{:S(2)}) async-start(), calls=%async_computation.4 | async-start | bytes 4718592 | tf_op jit(solution)/shard_map/all_gather | solution.py:335
  62.5 20.7 %collective-permute-start.3 = (bf16[4,32,1536]{2,1,0:T(8,128)(2,1)S(1)}, bf16[4,32,1536]{2,1,0:T(8,128)(2,1)S(1)}, u32[]{:S(2)}, u32[]{:S(2)}) collective-permute-start(bf16[4,32,1536]{2,1,0:T(8,128)(2,1)S(1)} %constant_dynamic-slice_fusion), channel_id=1, source_target_pairs={{0,32},{32,0},{1,33},{33,1},{2,34},{34,2},{3,35},{35,3},{4,36},{36... | collective-permute-start | bytes 1179656 | tf_op jit(solution)/shard_map/ppermute | solution.py:54
  84.2 90.4 %all-gather.7.cloned.1.call-start = ((), (), s32[]{:S(2)}) async-start(), calls=%async_computation.5 | async-start | bytes 2359296 | tf_op jit(solution)/shard_map/all_gather | solution.py:343
  84.4 17.4 %collective-permute-start.6 = (bf16[1,256,640]{2,1,0:T(8,128)(2,1)S(1)}, bf16[1,256,640]{2,1,0:T(8,128)(2,1)S(1)}, u32[]{:S(2)}, u32[]{:S(2)}) collective-permute-start(bf16[1,256,640]{2,1,0:T(8,128)(2,1)S(1)} %bitcast.117), channel_id=1, source_target_pairs={{0,24},{8,0},{16,8},{24,16},{1,25},{9,1},{17,9},{25,17},{2,26},{10... | collective-permute-start | bytes 983048 | tf_op jit(solution)/shard_map/ppermute | solution.py:50
  84.4 17.3 %collective-permute-start.5 = (bf16[1,256,640]{2,1,0:T(8,128)(2,1)S(1)}, bf16[1,256,640]{2,1,0:T(8,128)(2,1)S(1)}, u32[]{:S(2)}, u32[]{:S(2)}) collective-permute-start(bf16[1,256,640]{2,1,0:T(8,128)(2,1)S(1)} %bitcast.118), channel_id=1, source_target_pairs={{0,16},{8,24},{16,0},{24,8},{1,17},{9,25},{17,1},{25,9},{2,18},{10... | collective-permute-start | bytes 983048 | tf_op jit(solution)/shard_map/ppermute | solution.py:50
  86.4 16.0 %collective-permute-start.4 = (bf16[1,256,640]{2,1,0:T(8,128)(2,1)S(1)}, bf16[1,256,640]{2,1,0:T(8,128)(2,1)S(1)}, u32[]{:S(2)}, u32[]{:S(2)}) collective-permute-start(bf16[1,256,640]{2,1,0:T(8,128)(2,1)S(1)} %bitcast.119), channel_id=1, source_target_pairs={{0,8},{8,16},{16,24},{24,0},{1,9},{9,17},{17,25},{25,1},{2,10},{10... | collective-permute-start | bytes 983048 | tf_op jit(solution)/shard_map/ppermute | solution.py:50
  87.7 16.3 %collective-permute-start.9 = (bf16[1,256,640]{2,1,0:T(8,128)(2,1)S(1)}, bf16[1,256,640]{2,1,0:T(8,128)(2,1)S(1)}, u32[]{:S(2)}, u32[]{:S(2)}) collective-permute-start(bf16[1,256,640]{2,1,0:T(8,128)(2,1)S(1)} %bitcast.114), channel_id=1, source_target_pairs={{0,32},{32,0},{1,33},{33,1},{2,34},{34,2},{3,35},{35,3},{4,36},{36... | collective-permute-start | bytes 983048 | tf_op jit(solution)/shard_map/ppermute | solution.py:54
  103.7 36.3 %collective-permute-start.7 = (bf16[4,256,640]{2,1,0:T(8,128)(2,1)}, bf16[4,256,640]{2,1,0:T(8,128)(2,1)}, u32[]{:S(2)}, u32[]{:S(2)}) collective-permute-start(bf16[4,256,640]{2,1,0:T(8,128)(2,1)} %pad_maximum_fusion), channel_id=1, source_target_pairs={{0,32},{32,0},{1,33},{33,1},{2,34},{34,2},{3,35},{35,3},{4,36},{36... | collective-permute-start | bytes 3932168 | tf_op jit(solution)/shard_map/ppermute | solution.py:54
  104.1 30.6 %collective-permute-start.10 = (bf16[2,256,640]{2,1,0:T(8,128)(2,1)S(1)}, bf16[2,256,640]{2,1,0:T(8,128)(2,1)}, u32[]{:S(2)}, u32[]{:S(2)}) collective-permute-start(bf16[2,256,640]{2,1,0:T(8,128)(2,1)S(1)} %pad_maximum_fusion.1), channel_id=1, source_target_pairs={{0,8},{8,16},{16,24},{24,0},{1,9},{9,17},{17,25},{25,1},{2,10},{10... | collective-permute-start | bytes 1966088 | tf_op jit(solution)/shard_map/ppermute | solution.py:50
  107.4 29.2 %collective-permute-start.11 = (bf16[2,256,640]{2,1,0:T(8,128)(2,1)S(1)}, bf16[2,256,640]{2,1,0:T(8,128)(2,1)}, u32[]{:S(2)}, u32[]{:S(2)}) collective-permute-start(bf16[2,256,640]{2,1,0:T(8,128)(2,1)S(1)} %pad_maximum_fusion.1), channel_id=1, source_target_pairs={{0,16},{8,24},{16,0},{24,8},{1,17},{9,25},{17,1},{25,9},{2,18},{10... | collective-permute-start | bytes 1966088 | tf_op jit(solution)/shard_map/ppermute | solution.py:50
  110.1 29.0 %collective-permute-start.12 = (bf16[2,256,640]{2,1,0:T(8,128)(2,1)S(1)}, bf16[2,256,640]{2,1,0:T(8,128)(2,1)S(1)}, u32[]{:S(2)}, u32[]{:S(2)}) collective-permute-start(bf16[2,256,640]{2,1,0:T(8,128)(2,1)S(1)} %pad_maximum_fusion.1), channel_id=1, source_target_pairs={{0,24},{8,0},{16,8},{24,16},{1,25},{9,1},{17,9},{25,17},{2,26},{10... | collective-permute-start | bytes 1966088 | tf_op jit(solution)/shard_map/ppermute | solution.py:50
  140.0 9.6 %collective-permute-start.13 = (bf16[8,256,640]{2,1,0:T(8,128)(2,1)}, bf16[8,256,640]{2,1,0:T(8,128)(2,1)}, u32[]{:S(2)}, u32[]{:S(2)}) collective-permute-start(bf16[8,256,640]{2,1,0:T(8,128)(2,1)} %constant_dynamic-update-slice_fusion.12.b_own), channel_id=1, source_target_pairs={{0,64},{64,0},{1,65},{65,1},{2,66},{66,2},{3,67},{67,3},{4,68},{68... | collective-permute-start | bytes 7864328 | tf_op jit(solution)/shard_map/ppermute | solution.py:54
  142.5 7.1 %collective-permute-start.8 = (bf16[8,256,640]{2,1,0:T(8,128)(2,1)}, bf16[8,256,640]{2,1,0:T(8,128)(2,1)}, u32[]{:S(2)}, u32[]{:S(2)}) collective-permute-start(bf16[8,256,640]{2,1,0:T(8,128)(2,1)} %constant_dynamic-update-slice_fusion.7.a_own), channel_id=1, source_target_pairs={{0,64},{64,0},{1,65},{65,1},{2,66},{66,2},{3,67},{67,3},{4,68},{68... | collective-permute-start | bytes 7864328 | tf_op jit(solution)/shard_map/ppermute | solution.py:54
  177.1 2.0 collective-permute-start.14
  179.2 26.5 %copy-start.1 = (bf16[1,2048,352]{1,2,0:T(8,128)(2,1)S(1)}, bf16[1,2048,352]{1,2,0:T(8,128)(2,1)}, u32[]{:S(2)}) copy-start(bf16[1,2048,352]{1,2,0:T(8,128)(2,1)} %param.26) | copy-start | bytes 4325380
  179.3 8.4 %collective-permute-start.15 = (f32[128,512]{1,0:T(8,128)S(1)}, f32[128,512]{1,0:T(8,128)S(1)}, u32[]{:S(2)}, u32[]{:S(2)}) collective-permute-start(f32[128,512]{1,0:T(8,128)S(1)} %dynamic-slice_bitcast_fusion.1), channel_id=1, source_target_pairs={{0,128},{128,0},{1,129},{129,1},{2,130},{130,2},{3,131},{131,3},{4... | collective-permute-start | bytes 786440 | tf_op jit(solution)/shard_map/ppermute | solution.py:54
  194.5 40.3 %all-to-all-start.2 = ((bf16[128,8,512]{2,1,0:T(8,128)(2,1)}), bf16[128,8,512]{2,1,0:T(8,128)(2,1)S(1)}, u32[]{:S(2)}, u32[]{:S(2)}) async-start(bf16[128,8,512]{2,1,0:T(8,128)(2,1)} %fusion.2), calls=%async_computation.2 | async-start | bytes 2097152 | tf_op jit(solution)/shard_map/all_to_all | solution.py:458
  205.7 44.6 %collective-permute-start.17 = (bf16[352,2048]{1,0:T(8,128)(2,1)S(1)}, bf16[352,2048]{1,0:T(8,128)(2,1)}, u32[]{:S(2)}, u32[]{:S(2)}) collective-permute-start(bf16[352,2048]{1,0:T(8,128)(2,1)S(1)} %bitcast.104), channel_id=1, source_target_pairs={{0,128},{128,0},{1,129},{129,1},{2,130},{130,2},{3,131},{131,3},{4... | collective-permute-start | bytes 4325384 | tf_op jit(solution)/shard_map/ppermute | solution.py:54
  207.7 73.5 %collective-permute-start.18 = (bf16[352,2048]{1,0:T(8,128)(2,1)}, bf16[352,2048]{1,0:T(8,128)(2,1)}, u32[]{:S(2)}, u32[]{:S(2)}) collective-permute-start(bf16[352,2048]{1,0:T(8,128)(2,1)} %bitcast.106), channel_id=1, source_target_pairs={{0,128},{128,0},{1,129},{129,1},{2,130},{130,2},{3,131},{131,3},{4... | collective-permute-start | bytes 4325384 | tf_op jit(solution)/shard_map/ppermute | solution.py:54
  207.9 104.0 %collective-permute-start.19 = (bf16[352,2048]{1,0:T(8,128)(2,1)}, bf16[352,2048]{1,0:T(8,128)(2,1)}, u32[]{:S(2)}, u32[]{:S(2)}) collective-permute-start(bf16[352,2048]{1,0:T(8,128)(2,1)} %bitcast.135), channel_id=1, source_target_pairs={{0,128},{128,0},{1,129},{129,1},{2,130},{130,2},{3,131},{131,3},{4... | collective-permute-start | bytes 4325384 | tf_op jit(solution)/shard_map/ppermute | solution.py:54
  234.8 77.1 %collective-permute-start.16 = (bf16[2,512,512]{2,1,0:T(8,128)(2,1)S(1)}, bf16[2,512,512]{2,1,0:T(8,128)(2,1)S(1)}, u32[]{:S(2)}, u32[]{:S(2)}) collective-permute-start(bf16[2,512,512]{2,1,0:T(8,128)(2,1)S(1)} %bitcast.101), channel_id=1, source_target_pairs={{0,64},{64,0},{1,65},{65,1},{2,66},{66,2},{3,67},{67,3},{4,68},{68... | collective-permute-start | bytes 3145736 | tf_op jit(solution)/shard_map/ppermute | solution.py:54
  324.6 2.7 collective-permute-start.20
  330.2 42.0 %all-to-all-start.3 = ((bf16[128,8,512]{2,1,0:T(8,128)(2,1)}), bf16[128,8,512]{2,1,0:T(8,128)(2,1)S(1)}, u32[]{:S(2)}, u32[]{:S(2)}) async-start(bf16[128,8,512]{2,1,0:T(8,128)(2,1)} %bitcast.54), calls=%async_computation.3 | async-start | bytes 2097152 | tf_op jit(solution)/shard_map/all_to_all | solution.py:467
  (12 other events, 118.0 us)
Sparse Core Ops, SparseCore 0:
  84.4 47.4 all-gather.4
  133.6 40.9 all-gather.6
